TPU v7x, 32 devices: a whole 2x2x4 slice. The times are simulated.
32 devices in a mesh: ctx: 8 (over y, x, core), wa: 4 (over z).
Axes of the slice: x: 2, y: 2, z: 4, core: 2. Of those that a mesh axis runs over, the one named last changes fastest.
Arguments:
- tokens: bfloat16 [8, 1024, 768], P('wa', 'ctx'), may hold values from -6 to 6
- doc_lengths: int32 [8], replicated, may hold values from 256 to 1024, as said below
- group_deal: int32 [8, 8], replicated, may hold values from 0 to 7, each once within a row
- qkv_weight: bfloat16 [768, 2304], P('wa'), may hold values from -0.21875 to 0.21875
- out_weight: bfloat16 [768, 768], P('wa'), may hold values from -2.5 to 2.5
- up_weight: bfloat16 [768, 3072], P('wa'), may hold values from -0.21875 to 0.21875
- up_bias: bfloat16 [3072], P('wa'), may hold values from -3 to 3
- down_weight: bfloat16 [3072, 768], P('wa'), may hold values from -0.109375 to 0.109375
- proj_weight: bfloat16 [768, 128], P('wa'), may hold values from -0.21875 to 0.21875
- vectors: bfloat16 [8, 768], P(None, 'wa'), may hold values from -2 to 2
- cotangent: bfloat16 [8, 1024, 128], P('wa', 'ctx'), may hold values from -6 to 6
Outputs:
- embeddings: bfloat16 [8, 1024, 128], P('wa', 'ctx')
- tokens_grad: float32 [8, 1024, 768], P('wa', 'ctx')
- qkv_grad: float32 [768, 2304], P('wa')
- out_grad: float32 [768, 768], P('wa')
- up_grad: float32 [768, 3072], P('wa')
- bias_grad: float32 [3072], P('wa')
- down_grad: float32 [3072, 768], P('wa')
- proj_grad: float32 [768, 128], P('wa')
- vectors_grad: float32 [8, 768], P(None, 'wa')
Inputs may be any that keep to these rules, and one draw needn't show every extreme that they name: `doc_lengths`: every draw has a sequence with all 1024 slots valid. `group_deal`: each row is a permutation of the block numbers of a sequence.
All inputs are finite; a program needn't handle non-finite values.
Results may differ from a plain program's by a relative error of at most 0.023.
Values may be sent and summed in bfloat16 or wider, within the bound.
No kernel may reach another device: no remote copies, remote signals or barrier semaphores. Data moves between devices by JAX's collectives and lax.ppermute only.
A program may use at most 256 MiB of HBM per device.

v0:
```python
from functools import partial
import jax
import jax.numpy as jnp
from jax import lax
from jax.sharding import PartitionSpec as P

H = 12
HEAD = 64
NEG_FILL = -1e30
NORM_EPS = 1e-06
ROOT_HALF = 0.7071067811865476
DENSITY_SCALE = 0.3989422804014327


def norm_rows(inputs, gain_row, shift_row):
    middle = jnp.mean(inputs, axis=-1, keepdims=True)
    center = inputs - middle
    spread = jnp.mean(center * center, axis=-1, keepdims=True)
    scaled = lax.rsqrt(spread + NORM_EPS)
    unit_rows = center * scaled
    return (unit_rows * gain_row + shift_row, unit_rows, scaled)


def norm_back(grad_in, unit_rows, scaled, gain_row):
    gain_grad = jnp.sum(grad_in * unit_rows, axis=(0, 1))
    shift_grad = jnp.sum(grad_in, axis=(0, 1))
    inner_grad = grad_in * gain_row
    centered = inner_grad - jnp.mean(inner_grad, axis=-1, keepdims=True)
    result = scaled * (
        centered - unit_rows * jnp.mean(inner_grad * unit_rows, axis=-1, keepdims=True)
    )
    return (result, gain_grad, shift_grad)


def gelu_both(inner_sum):
    normal_cdf = 0.5 * (1.0 + lax.erf(inner_sum * ROOT_HALF))
    density = jnp.exp(-0.5 * inner_sum * inner_sum) * DENSITY_SCALE
    return (inner_sum * normal_cdf, normal_cdf + inner_sum * density)


def split_tiles(key_rows, value_rows, key_valid):
    key_count = key_rows.shape[0]
    tile_width = 512
    tile_count = key_count // tile_width
    return (
        key_rows.reshape(tile_count, tile_width, H, HEAD),
        value_rows.reshape(tile_count, tile_width, H, HEAD),
        key_valid.reshape(tile_count, tile_width),
    )


def masked_scores(queries, key_tile, mask_tile):
    products = jnp.einsum("qhd,khd->hqk", queries, key_tile, preferred_element_type=jnp.float32)
    return jnp.where(mask_tile[None, None, :], products, NEG_FILL)


def attend_forward(queries, key_rows, value_rows, key_valid):
    key_tiles, value_tiles, mask_tiles = split_tiles(key_rows, value_rows, key_valid)
    row_span = queries.shape[0]

    def stats_step(running, portion):
        highest, summed = running
        key_tile, mask_tile = portion
        scores = masked_scores(queries, key_tile, mask_tile)
        new_peak = jnp.maximum(highest, jnp.max(scores, axis=-1))
        raised = jnp.where(mask_tile[None, None, :], jnp.exp(scores - new_peak[:, :, None]), 0.0)
        return ((new_peak, summed * jnp.exp(highest - new_peak) + jnp.sum(raised, axis=-1)), None)

    start_peak = jnp.full((H, row_span), NEG_FILL, jnp.float32)
    start_sum = jnp.zeros((H, row_span), jnp.float32)
    (highest, summed), _ = lax.scan(stats_step, (start_peak, start_sum), (key_tiles, mask_tiles))
    logsum = highest + jnp.log(summed)

    def value_step(running, portion):
        key_tile, value_tile, mask_tile = portion
        scores = masked_scores(queries, key_tile, mask_tile)
        prob_low = jnp.where(
            mask_tile[None, None, :], jnp.exp(scores - logsum[:, :, None]), 0.0
        ).astype(jnp.bfloat16)
        return (
            running
            + jnp.einsum("hqk,khd->qhd", prob_low, value_tile, preferred_element_type=jnp.float32),
            None,
        )

    attended, _ = lax.scan(
        value_step,
        jnp.zeros((row_span, H, HEAD), jnp.float32),
        (key_tiles, value_tiles, mask_tiles),
    )
    return (attended, logsum)


def attend_backward(
    queries, key_rows, value_rows, key_valid, logsum, delta_rows, grad_heads, with_keys
):
    key_tiles, value_tiles, mask_tiles = split_tiles(key_rows, value_rows, key_valid)

    def back_step(running, portion):
        key_tile, value_tile, mask_tile = portion
        scores = masked_scores(queries, key_tile, mask_tile)
        prob_rows = jnp.where(mask_tile[None, None, :], jnp.exp(scores - logsum[:, :, None]), 0.0)
        prob_grad = jnp.einsum(
            "qhd,khd->hqk", grad_heads, value_tile, preferred_element_type=jnp.float32
        )
        score_low = (prob_rows * (prob_grad - delta_rows[:, :, None])).astype(jnp.bfloat16)
        running = running + jnp.einsum(
            "hqk,khd->qhd", score_low, key_tile, preferred_element_type=jnp.float32
        )
        value_part = jnp.einsum(
            "hqk,qhd->khd",
            prob_rows.astype(jnp.bfloat16),
            grad_heads,
            preferred_element_type=jnp.float32,
        )
        key_part = jnp.einsum(
            "hqk,qhd->khd", score_low, queries, preferred_element_type=jnp.float32
        )
        return (running, (key_part, value_part))

    start_grad = jnp.zeros(queries.shape, jnp.float32)
    query_grad, pieces = lax.scan(back_step, start_grad, (key_tiles, value_tiles, mask_tiles))
    key_count = key_rows.shape[0]
    return (
        query_grad,
        pieces[0].reshape(key_count, H * HEAD),
        pieces[1].reshape(key_count, H * HEAD),
    )


def body(
    tokens,
    doc_lengths,
    group_deal,
    qkv_weight,
    out_weight,
    up_weight,
    up_bias,
    down_weight,
    proj_weight,
    vectors,
    cotangent,
):
    gathered = (
        lax.all_gather(qkv_weight, "wa", axis=0, tiled=True),
        lax.all_gather(out_weight, "wa", axis=0, tiled=True),
        lax.all_gather(up_weight, "wa", axis=0, tiled=True),
        lax.all_gather(up_bias, "wa", axis=0, tiled=True),
        lax.all_gather(down_weight, "wa", axis=0, tiled=True),
        lax.all_gather(proj_weight, "wa", axis=0, tiled=True),
        lax.all_gather(vectors, "wa", axis=1, tiled=True),
    )
    qkv_full, out_full, up_full, bias_full, down_full, proj_full, vector_full = gathered
    seq_count, group_rows, model_width = tokens.shape
    ctx_count = lax.axis_size("ctx")
    seq_start = lax.axis_index("wa") * seq_count
    my_lengths = lax.dynamic_slice_in_dim(doc_lengths, seq_start, seq_count, 0)
    my_deal = lax.dynamic_slice_in_dim(group_deal, seq_start, seq_count, 0)
    offsets = jnp.tile(jnp.arange(group_rows, dtype=jnp.int32), ctx_count)
    positions = jnp.repeat(my_deal, group_rows, axis=1) * group_rows + offsets[None, :]
    key_valid = positions < my_lengths[:, None]
    query_valid = lax.dynamic_slice_in_dim(
        key_valid, lax.axis_index("ctx") * group_rows, group_rows, 1
    )
    row_mask = query_valid.astype(jnp.float32)[:, :, None]
    query_scale = HEAD ** (-0.5)
    mixed_rows = jnp.einsum("scd,de->sce", tokens, qkv_full, preferred_element_type=jnp.float32)
    queries = ((mixed_rows[:, :, :model_width] + vector_full[0]) * query_scale).astype(jnp.bfloat16)
    key_rows = mixed_rows[:, :, model_width : 2 * model_width].astype(jnp.bfloat16)
    value_rows = (mixed_rows[:, :, 2 * model_width :] + vector_full[1]).astype(jnp.bfloat16)
    all_keys, all_values = (
        lax.all_gather(key_rows, "ctx", axis=1, tiled=True),
        lax.all_gather(value_rows, "ctx", axis=1, tiled=True),
    )
    query_heads = queries.reshape(seq_count, group_rows, H, HEAD)
    attended, logsum = jax.vmap(attend_forward)(query_heads, all_keys, all_values, key_valid)
    attended_low = attended.reshape(seq_count, group_rows, model_width).astype(jnp.bfloat16)
    first_sum = tokens.astype(jnp.float32) + (
        jnp.einsum("scd,de->sce", attended_low, out_full, preferred_element_type=jnp.float32)
        + vector_full[2]
    )
    normed, unit_one, scale_one = norm_rows(first_sum, vector_full[3], vector_full[4])
    normed_low = normed.astype(jnp.bfloat16)
    inner_sum = (
        jnp.einsum("scd,df->scf", normed_low, up_full, preferred_element_type=jnp.float32)
        + bias_full
    )
    active, gelu_slope = gelu_both(inner_sum)
    active_low = active.astype(jnp.bfloat16)
    second_sum = normed + (
        jnp.einsum("scf,fd->scd", active_low, down_full, preferred_element_type=jnp.float32)
        + vector_full[5]
    )
    final_sum, unit_two, scale_two = norm_rows(second_sum, vector_full[6], vector_full[7])
    final_low = final_sum.astype(jnp.bfloat16)
    project = jnp.einsum("scd,de->sce", final_low, proj_full, preferred_element_type=jnp.float32)
    inverse = lax.rsqrt(jnp.sum(project * project, axis=-1, keepdims=True) + NORM_EPS)
    direction = project * inverse
    embeddings = (direction * row_mask).astype(jnp.bfloat16)
    upstream = cotangent.astype(jnp.float32) * row_mask
    project_grad = (
        inverse * (upstream - direction * jnp.sum(upstream * direction, axis=-1, keepdims=True))
    ).astype(jnp.bfloat16)
    proj_grad = jnp.einsum(
        "scd,sce->de", final_low, project_grad, preferred_element_type=jnp.float32
    )
    final_grad = jnp.einsum(
        "sce,de->scd", project_grad, proj_full, preferred_element_type=jnp.float32
    )
    second_grad, gain_two, shift_two = norm_back(final_grad, unit_two, scale_two, vector_full[6])
    down_low = second_grad.astype(jnp.bfloat16)
    down_grad = jnp.einsum("scf,scd->fd", active_low, down_low, preferred_element_type=jnp.float32)
    inner_grad = (
        jnp.einsum("scd,fd->scf", down_low, down_full, preferred_element_type=jnp.float32)
        * gelu_slope
    )
    bias_grad = jnp.sum(inner_grad, axis=(0, 1))
    inner_low = inner_grad.astype(jnp.bfloat16)
    up_grad = jnp.einsum("scd,scf->df", normed_low, inner_low, preferred_element_type=jnp.float32)
    normed_grad = second_grad + jnp.einsum(
        "scf,df->scd", inner_low, up_full, preferred_element_type=jnp.float32
    )
    first_grad, gain_one, shift_one = norm_back(normed_grad, unit_one, scale_one, vector_full[3])
    first_low = first_grad.astype(jnp.bfloat16)
    out_grad = jnp.einsum(
        "scd,sce->de", attended_low, first_low, preferred_element_type=jnp.float32
    )
    attended_grad = jnp.einsum(
        "sce,de->scd", first_low, out_full, preferred_element_type=jnp.float32
    ).astype(jnp.bfloat16)
    grad_heads = attended_grad.reshape(seq_count, group_rows, H, HEAD)
    delta_rows = jnp.sum(grad_heads.astype(jnp.float32) * attended, axis=-1)
    delta_heads = jnp.swapaxes(delta_rows, 1, 2)
    query_grad, key_terms, value_terms = jax.vmap(partial(attend_backward, with_keys=True))(
        query_heads, all_keys, all_values, key_valid, logsum, delta_heads, grad_heads
    )
    key_grad, value_grad = (
        lax.psum_scatter(
            key_terms.astype(jnp.bfloat16), "ctx", scatter_dimension=1, tiled=True
        ).astype(jnp.float32),
        lax.psum_scatter(
            value_terms.astype(jnp.bfloat16), "ctx", scatter_dimension=1, tiled=True
        ).astype(jnp.float32),
    )
    query_part = (
        query_grad.reshape(seq_count, group_rows, model_width).astype(jnp.bfloat16) * query_scale
    )
    value_part = value_grad.astype(jnp.bfloat16)
    mixed_grad = jnp.concatenate([query_part, key_grad.astype(jnp.bfloat16), value_part], axis=-1)
    qkv_grad = jnp.einsum("scd,sce->de", tokens, mixed_grad, preferred_element_type=jnp.float32)
    tokens_grad = first_grad + jnp.einsum(
        "sce,de->scd", mixed_grad, qkv_full, preferred_element_type=jnp.float32
    )
    vectors_grad = jnp.stack(
        [
            jnp.sum(query_part.astype(jnp.float32), axis=(0, 1)),
            jnp.sum(value_part.astype(jnp.float32), axis=(0, 1)),
            jnp.sum(first_grad, axis=(0, 1)),
            gain_one,
            shift_one,
            jnp.sum(second_grad, axis=(0, 1)),
            gain_two,
            shift_two,
        ],
        axis=0,
    )
    owned = (
        lax.psum_scatter(
            qkv_grad.astype(jnp.bfloat16), "wa", scatter_dimension=0, tiled=True
        ).astype(jnp.float32),
        lax.psum_scatter(
            out_grad.astype(jnp.bfloat16), "wa", scatter_dimension=0, tiled=True
        ).astype(jnp.float32),
        lax.psum_scatter(
            up_grad.astype(jnp.bfloat16), "wa", scatter_dimension=0, tiled=True
        ).astype(jnp.float32),
        lax.psum_scatter(
            bias_grad.astype(jnp.bfloat16), "wa", scatter_dimension=0, tiled=True
        ).astype(jnp.float32),
        lax.psum_scatter(
            down_grad.astype(jnp.bfloat16), "wa", scatter_dimension=0, tiled=True
        ).astype(jnp.float32),
        lax.psum_scatter(
            proj_grad.astype(jnp.bfloat16), "wa", scatter_dimension=0, tiled=True
        ).astype(jnp.float32),
        lax.psum_scatter(
            vectors_grad.astype(jnp.bfloat16), "wa", scatter_dimension=1, tiled=True
        ).astype(jnp.float32),
    )
    summed = (
        lax.psum(owned[0].astype(jnp.bfloat16), "ctx").astype(jnp.float32),
        lax.psum(owned[1].astype(jnp.bfloat16), "ctx").astype(jnp.float32),
        lax.psum(owned[2].astype(jnp.bfloat16), "ctx").astype(jnp.float32),
        lax.psum(owned[3].astype(jnp.bfloat16), "ctx").astype(jnp.float32),
        lax.psum(owned[4].astype(jnp.bfloat16), "ctx").astype(jnp.float32),
        lax.psum(owned[5].astype(jnp.bfloat16), "ctx").astype(jnp.float32),
        lax.psum(owned[6].astype(jnp.bfloat16), "ctx").astype(jnp.float32),
    )
    return (
        embeddings,
        tokens_grad,
        summed[0],
        summed[1],
        summed[2],
        summed[3],
        summed[4],
        summed[5],
        summed[6],
    )


def solution(mesh):
    in_specs = (
        P("wa", "ctx", None),
        P(),
        P(),
        P("wa", None),
        P("wa", None),
        P("wa", None),
        P("wa"),
        P("wa", None),
        P("wa", None),
        P(None, "wa"),
        P("wa", "ctx", None),
    )
    out_specs = (
        P("wa", "ctx", None),
        P("wa", "ctx", None),
        P("wa", None),
        P("wa", None),
        P("wa", None),
        P("wa"),
        P("wa", None),
        P("wa", None),
        P(None, "wa"),
    )
    return jax.shard_map(body, mesh=mesh, in_specs=in_specs, out_specs=out_specs, check_vma=False)
```

profile of v0, /device:TPU:0, one launch (start us, length us, event | category | flops | bytes accessed | tf_op | source)
XLA Modules:
  0.0 944.5 jit_solution(11446303625677070540)
XLA Ops:
  8.0 15.1 %all-gather = bf16[4,192,8]{1,2,0:T(8,128)(2,1)S(1)} all-gather(bf16[1,192,8]{1,2,0:T(8,128)(2,1)} %bitcast.249), channel_id=1, replica_groups=mesh['ctx'=8,'wa'=4] {'wa'}, dimensions={0}, use_global_device_ids=true | all-gather | bytes 15360 | tf_op jit(solution)/shard_map/all_gather | solution.py:151
  23.8 58.5 %all-gather.9.cloned.1.call-done = bf16[768,2304]{1,0:T(8,128)(2,1)} async-done(((bf16[192,2304]{1,0:T(8,128)(2,1)}), bf16[768,2304]{1,0:T(8,128)(2,1)}) %all-gather.9.cloned.1.call-update) | async-done | bytes 3538960 | tf_op jit(solution)/shard_map/all_gather | solution.py:145
  82.3 3.2 fusion.81
  90.8 13.1 %all-gather.1 = bf16[4,1,768]{2,1,0:T(2,128)(2,1)S(1)} all-gather(bf16[1,1,768]{2,1,0:T(2,128)(2,1)S(1)} %reshape.193), channel_id=1, replica_groups=mesh['ctx'=8,'wa'=4] {'wa'}, dimensions={0}, use_global_device_ids=true | all-gather | bytes 7680 | tf_op jit(solution)/shard_map/all_gather | solution.py:148
  105.4 14.3 %all_gather.35 = bf16[768,128]{1,0:T(8,128)(2,1)} all-gather(bf16[192,128]{1,0:T(8,128)(2,1)S(1)} %copy-done.36), channel_id=1, replica_groups=mesh['ctx'=8,'wa'=4] {'wa'}, dimensions={0}, use_global_device_ids=true | all-gather | bytes 245760 | tf_op jit(solution)/shard_map/all_gather | solution.py:150
  120.6 3.2 copy.70
  123.8 4.0 reshape.179
  127.8 4.3 copy.75
  132.1 19.9 %all-gather.13.cloned.1.call-done = bf16[2,1024,768]{2,1,0:T(8,128)(2,1)} async-done(((bf16[2,128,768]{2,1,0:T(8,128)(2,1)}), bf16[2,1024,768]{2,1,0:T(8,128)(2,1)}) %all-gather.13.cloned.1.call-update) | async-done | bytes 3145744 | tf_op jit(solution)/shard_map/all_gather | solution.py:172
  152.0 3.2 copy.71
  155.2 4.0 reshape.180
  159.2 2.7 copy.77
  162.0 8.7 while.39
  172.0 11.2 %while.40 = (s32[]{:T(128)}, f32[2,128,12,64]{1,3,2,0:T(8,128)}, bf16[2,2,512,12,64]{2,4,3,1,0:T(8,128)(2,1)}, pred[2,2,512]{2,1,0:T(4,128)(4,1)}, bf16[2,2,512,...) while((s32[]{:T(128)}, f32[2,128,12,64]{1,3,2,0:T(8,128)}, ...), condition=%wide.region_5.6_spmd.clone, body=%wide.region_4.5_spmd.clone.sunk | while | flops 409337856 | bytes 5133938 | solution.py:86
  172.6 4.6 fusion.200
  177.9 4.8 fusion.200
  188.4 85.4 %all-gather.17.cloned.1.call-done = bf16[768,3072]{1,0:T(8,128)(2,1)} async-done(((bf16[192,3072]{1,0:T(8,128)(2,1)}), bf16[768,3072]{1,0:T(8,128)(2,1)}) %all-gather.17.cloned.1.call-update) | async-done | bytes 4718608 | tf_op jit(solution)/shard_map/all_gather | solution.py:147
  273.8 6.5 multiply_convert_fusion.1
  280.4 82.7 %all-gather.19.cloned.1.call-done = bf16[3072,768]{1,0:T(8,128)(2,1)} async-done(((bf16[768,768]{1,0:T(8,128)(2,1)}), bf16[3072,768]{1,0:T(8,128)(2,1)}) %all-gather.19.cloned.1.call-update) | async-done | bytes 4718608 | tf_op jit(solution)/shard_map/all_gather | solution.py:149
  363.1 4.5 fusion.155
  370.2 3.2 multiply_reduce_fusion
  376.6 7.2 fusion.158
  393.8 25.8 %while.41 = (s32[]{:T(128)}, f32[2,128,12,64]{1,3,2,0:T(8,128)}, bf16[2,2,512,12,64]{2,4,3,1,0:T(8,128)(2,1)}, bf16[2,2,512,12,64]{2,4,3,1,0:T(8,128)(2,1)}, bf1...) while((s32[]{:T(128)}, f32[2,128,12,64]{1,3,2,0:T(8,128)}, ...), condition=%wide.region_18.19_spmd.clone, body=%wide.region_17.18_spmd.clone.sunk | while | flops 1022754816 | bytes 113400248 | solution.py:122
  395.9 2.7 multiply_convert_fusion.4
  408.7 2.7 multiply_convert_fusion.4
  419.6 5.1 copy.87
  424.7 3.9 convert_element_type.275
  428.6 4.7 copy.88
  433.6 5.1 copy.85
  438.7 3.9 convert_element_type.272
  442.6 4.7 copy.86
  450.2 27.7 %reduce-scatter.15.cloned.1.call-done = bf16[2,128,768]{2,1,0:T(8,128)(2,1)} async-done(((bf16[2,1024,768]{2,1,0:T(8,128)(2,1)}), bf16[2,128,768]{2,1,0:T(8,128)(2,1)}) %reduce-scatter.15.cloned.1.call-update) | async-done | bytes 393232 | tf_op jit(solution)/shard_map/reduce_scatter | solution.py:241
  477.9 49.4 %reduce-scatter.13.cloned.1.call-done = bf16[2,128,768]{2,1,0:T(8,128)(2,1)} async-done(((bf16[2,1024,768]{2,1,0:T(8,128)(2,1)}), bf16[2,128,768]{2,1,0:T(8,128)(2,1)}) %reduce-scatter.13.cloned.1.call-update) | async-done | bytes 393232 | tf_op jit(solution)/shard_map/reduce_scatter | solution.py:238
  527.3 2.5 fusion.72
  529.8 4.0 copy.104
  536.7 4.5 bitcast_convert_fusion.1
  542.8 3.6 bitcast_convert_fusion
  550.7 49.9 %reduce-scatter.25.cloned.1.call-done = bf16[192,2304]{1,0:T(8,128)(2,1)} async-done(((bf16[768,2304]{1,0:T(8,128)(2,1)}), bf16[192,2304]{1,0:T(8,128)(2,1)}) %reduce-scatter.25.cloned.1.call-update) | async-done | bytes 884752
  602.9 29.9 %reduce-scatter.17.cloned.1.call-done = bf16[192,768]{1,0:T(8,128)(2,1)} async-done(((bf16[768,768]{1,0:T(8,128)(2,1)}), bf16[192,768]{1,0:T(8,128)(2,1)}) %reduce-scatter.17.cloned.1.call-update) | async-done | bytes 294928 | tf_op jit(solution)/shard_map/reduce_scatter | solution.py:271
  632.8 86.2 %reduce-scatter.19.cloned.1.call-done = bf16[192,3072]{1,0:T(8,128)(2,1)} async-done(((bf16[768,3072]{1,0:T(8,128)(2,1)}), bf16[192,3072]{1,0:T(8,128)(2,1)}) %reduce-scatter.19.cloned.1.call-update) | async-done | bytes 1179664 | tf_op jit(solution)/shard_map/reduce_scatter | solution.py:274
  719.0 88.0 %reduce-scatter.21.cloned.1.call-done = bf16[768,768]{1,0:T(8,128)(2,1)} async-done(((bf16[3072,768]{1,0:T(8,128)(2,1)}), bf16[768,768]{1,0:T(8,128)(2,1)}) %reduce-scatter.21.cloned.1.call-update) | async-done | bytes 1179664 | tf_op jit(solution)/shard_map/reduce_scatter | solution.py:280
  809.1 11.1 %all-reduce = bf16[3072]{0:T(1024)(128)(2,1)S(1)} all-reduce(bf16[3072]{0:T(1024)(128)(2,1)S(1)} %copy-done.54), channel_id=7, replica_groups=mesh['ctx'=8,'wa'=4] {'wa'}, use_global_device_ids=true, to_apply=%region_28.29.clone | all-reduce | flops 3072 | bytes 12288
  820.3 4.0 fusion.88
  824.3 5.8 reduce-scatter.27.cloned.1.call-done
  830.9 19.6 %reduce-scatter.23.cloned.1.call-done = bf16[192,128]{1,0:T(8,128)(2,1)} async-done(((bf16[768,128]{1,0:T(8,128)(2,1)}), bf16[192,128]{1,0:T(8,128)(2,1)}) %reduce-scatter.23.cloned.1.call-update) | async-done | bytes 49168 | tf_op jit(solution)/shard_map/reduce_scatter | solution.py:283
  850.5 24.6 %all-reduce.1 = (bf16[768]{0:T(1024)(128)(2,1)S(1)}, bf16[192,128]{1,0:T(8,128)(2,1)S(1)}, bf16[8,192]{1,0:T(8,128)(2,1)S(1)}) all-reduce(bf16[768]{0:T(1024)(128)(2,1)S(1)} %dynamic-slice.1, bf16[192,128]{1,0:T(8,128)(2,1)} %reduce-scatter.23.cloned.1.call-done, bf16[8,192]{1,0:T(8,128)(2,1)S(1)} %copy.107), channel_id=1, replica_groups=mesh['ctx'=8,'wa'=4] {'ctx'}, use_global_device_ids=true, to_apply=%region_29.30 | all-reduce | flops 26880 | bytes 107520 | tf_op jit(solution)/shard_map/psum | solution.py:294
  877.0 54.0 %all-reduce.5.cloned.1.call-done = (bf16[192,2304]{0,1:T(8,128)(2,1)}, bf16[192,768]{1,0:T(8,128)(2,1)}, bf16[192,3072]{1,0:T(8,128)(2,1)}, bf16[768,768]{1,0:T(8,128)(2,1)}) async-done(((bf16[192,2304]{0,1:T(8,128)(2,1)}, bf16[192,768]{1,0:T(8,128)(2,1)}, bf16[192,3072]{1,0:T(8,128)(2,1)}, bf16[768,768]{1,0:T(8,128)(2,1)}), (bf16[192,2304]{0,1:T(8,128)(2,1)}, bf16[192,768]{1,0:T(8,128)(2,1)}, ...) | async-done | bytes 3538960 | tf_op jit(solution)/shard_map/psum | solution.py:291
  931.0 2.6 copy.96
  (290 shorter events, 82.9 us)
Async XLA Ops:
  7.2 75.1 %all-gather.9.cloned.1.call-start = ((), (), s32[]{:S(2)}) async-start(), calls=%async_computation.8 | async-start | bytes 4423680 | tf_op jit(solution)/shard_map/all_gather | solution.py:145
  7.9 112.7 %all-gather.11.cloned.1.call-start = ((), (), s32[]{:S(2)}) async-start(), calls=%async_computation.9 | async-start | bytes 3538944 | tf_op jit(solution)/shard_map/all_gather | solution.py:173
  85.5 3.7 copy-start.57
  85.5 3.7 copy-start.63
  85.5 19.0 %copy-start.35 = (bf16[2,128,128]{2,1,0:T(8,128)(2,1)S(1)}, bf16[2,128,128]{2,1,0:T(8,128)(2,1)}, u32[]{:S(2)}) copy-start(bf16[2,128,128]{2,1,0:T(8,128)(2,1)} %param.27) | copy-start | bytes 196612
  85.5 19.9 %copy-start.36 = (bf16[192,128]{1,0:T(8,128)(2,1)S(1)}, bf16[192,128]{1,0:T(8,128)(2,1)}, u32[]{:S(2)}) copy-start(bf16[192,128]{1,0:T(8,128)(2,1)} %param.25) | copy-start | bytes 147460
  86.4 65.6 %all-gather.13.cloned.1.call-start = ((), (), s32[]{:S(2)}) async-start(), calls=%async_computation.10 | async-start | bytes 3538944 | tf_op jit(solution)/shard_map/all_gather | solution.py:172
  87.3 97.9 %all-gather.15.cloned.1.call-start = ((), (), s32[]{:S(2)}) async-start(), calls=%async_computation.11 | async-start | bytes 1474560 | tf_op jit(solution)/shard_map/all_gather | solution.py:146
  87.9 185.9 %all-gather.17.cloned.1.call-start = ((), (), s32[]{:S(2)}) async-start(), calls=%async_computation.12 | async-start | bytes 5898240 | tf_op jit(solution)/shard_map/all_gather | solution.py:147
  88.4 274.6 %all-gather.19.cloned.1.call-start = ((), (), s32[]{:S(2)}) async-start(), calls=%async_computation.13 | async-start | bytes 5898240 | tf_op jit(solution)/shard_map/all_gather | solution.py:149
  89.0 388.9 %reduce-scatter.15.cloned.1.call-start = ((), (), s32[]{:S(2)}) async-start(), calls=%async_computation.15 | async-start | bytes 3538944 | tf_op jit(solution)/shard_map/reduce_scatter | solution.py:241
  172.0 13.2 %copy-start.45 = (f32[768]{0:T(1024)S(1)}, f32[768]{0:T(1024)}, u32[]{:S(2)}) copy-start(f32[768]{0:T(1024)} %get-tuple-element.337) | copy-start | bytes 9220
  183.2 90.6 %copy-start.33 = (f32[768]{0:T(1024)S(1)}, f32[768]{0:T(1024)}, u32[]{:S(2)}) copy-start(f32[768]{0:T(1024)} %get-tuple-element.336) | copy-start | bytes 9220
  183.2 90.6 %copy-start.34 = (f32[768]{0:T(1024)S(1)}, f32[768]{0:T(1024)}, u32[]{:S(2)}) copy-start(f32[768]{0:T(1024)} %get-tuple-element.335) | copy-start | bytes 9220
  187.3 196.5 %copy-start.38 = (f32[2,128]{1,0:T(2,128)}, f32[2,128]{1,0:T(2,128)S(1)}, u32[]{:S(2)}) copy-start(f32[2,128]{1,0:T(2,128)S(1)} %broadcast_multiply_fusion.5) | copy-start | bytes 3076
  188.4 92.0 %copy-start.48 = (f32[2,128]{1,0:T(2,128)}, f32[2,128]{1,0:T(2,128)S(1)}, u32[]{:S(2)}) copy-start(f32[2,128]{1,0:T(2,128)S(1)} %add_rsqrt_fusion.2) | copy-start | bytes 3076
  363.1 5.5 copy-start.25
  363.1 5.5 copy-start.37
  363.1 5.5 copy-start.43
  374.2 9.6 %slice-start = ((s8[4718592]{0:T(1024)(128)(4,1)}), s8[4194304]{0:T(1024)(128)(4,1)S(1)}, s32[]{:S(2)}) async-start(s8[4718592]{0:T(1024)(128)(4,1)} %bitcast.250), calls=%async_computation.23 | async-start | bytes 8388608
  376.6 7.2 copy-start.18
  376.6 7.2 copy-start.4
  376.6 7.3 copy-start.49
  376.6 7.3 slice-start.1
  383.8 4.8 copy-start.10
  386.2 7.6 copy-start.31
  395.9 2.8 copy-start.13
  400.8 3.0 copy-start.15
  408.7 2.8 copy-start.13
  413.6 3.0 copy-start.15
  433.3 94.0 %reduce-scatter.13.cloned.1.call-start = ((), (), s32[]{:S(2)}) async-start(), calls=%async_computation.14 | async-start | bytes 3538944 | tf_op jit(solution)/shard_map/reduce_scatter | solution.py:238
  447.3 153.2 %reduce-scatter.25.cloned.1.call-start = ((), (), s32[]{:S(2)}) async-start(), calls=%async_computation.20 | async-start | bytes 4423680
  533.8 2.8 copy-start.5
  533.9 2.8 copy-start.22
  533.9 2.8 copy-start.39
  533.9 98.9 %reduce-scatter.17.cloned.1.call-start = ((), (), s32[]{:S(2)}) async-start(), calls=%async_computation.16 | async-start | bytes 1474560 | tf_op jit(solution)/shard_map/reduce_scatter | solution.py:271
  536.6 182.4 %reduce-scatter.19.cloned.1.call-start = ((), (), s32[]{:S(2)}) async-start(), calls=%async_computation.17 | async-start | bytes 5898240 | tf_op jit(solution)/shard_map/reduce_scatter | solution.py:274
  541.2 265.9 %reduce-scatter.21.cloned.1.call-start = ((), (), s32[]{:S(2)}) async-start(), calls=%async_computation.18 | async-start | bytes 5898240 | tf_op jit(solution)/shard_map/reduce_scatter | solution.py:280
  546.5 283.5 %reduce-scatter.27.cloned.1.call-start = ((), (), s32[]{:S(2)}) async-start(), calls=%async_computation.21 | async-start | bytes 245760
  548.4 302.1 %reduce-scatter.23.cloned.1.call-start = ((), (), s32[]{:S(2)}) async-start(), calls=%async_computation.19 | async-start | bytes 245760 | tf_op jit(solution)/shard_map/reduce_scatter | solution.py:283
  550.6 256.5 %copy-start.64 = (u32[32]{0:T(128)S(1)}, u32[32]{0:T(128)}, u32[]{:S(2)}) copy-start(u32[32]{0:T(128)} %constant.101) | copy-start | bytes 388
  550.6 258.5 %copy-start.54 = (bf16[3072]{0:T(1024)(128)(2,1)S(1)}, bf16[3072]{0:T(1024)(128)(2,1)}, u32[]{:S(2)}) copy-start(bf16[3072]{0:T(1024)(128)(2,1)} %get-tuple-element.415) | copy-start | bytes 18436
  550.6 269.7 %copy-start.30 = (bf16[2,128,768]{2,1,0:T(8,128)(2,1)S(1)}, bf16[2,128,768]{2,1,0:T(8,128)(2,1)}, u32[]{:S(2)}) copy-start(bf16[2,128,768]{2,1,0:T(8,128)(2,1)} %copy.89) | copy-start | bytes 1179652
  550.6 269.6 %copy-start.62 = (bf16[2,128,768]{2,1,0:T(8,128)(2,1)S(1)}, bf16[2,128,768]{2,1,0:T(8,128)(2,1)}, u32[]{:S(2)}) copy-start(bf16[2,128,768]{2,1,0:T(8,128)(2,1)} %reduce-scatter.13.cloned.1.call-done) | copy-start | bytes 1179652
  550.6 380.4 %all-reduce.5.cloned.1.call-start = ((), (), s32[]{:S(2)}) async-start(), calls=%async_computation.22 | async-start | bytes 7667712 | tf_op jit(solution)/shard_map/psum | solution.py:291
  931.0 2.6 copy-start.32
  931.0 3.5 copy-start.24
  931.0 5.2 copy-start.23
  (46 other events, 69.0 us)
Sparse Core Ops, SparseCore 0:
  9.6 72.6 all-gather.8
  86.5 30.7 all-gather.10
  119.8 32.1 all-gather.12
  153.4 30.2 all-gather.14
  185.2 88.6 all-gather.16
  275.2 87.7 all-gather.18
  433.4 44.4 reduce-scatter.14
  481.3 46.0 reduce-scatter.12
  534.0 66.4 reduce-scatter.24
  603.3 29.4 reduce-scatter.16
  635.1 83.8 reduce-scatter.18
  721.2 85.7 reduce-scatter.20
  809.9 20.1 reduce-scatter.26
  832.7 17.7 reduce-scatter.22
  854.7 76.2 all-reduce.4
where the time goes:
time: 953 us; the launch traced here: 945 us
  waiting for transfers between devices  660 us (69%)
  local copies, waits for them, and re-layouts  86.5 us (9%)
  matrix products  78.4 us (8%)
  blocking collectives  78.2 us (8%)
  other arithmetic  24.5 us (3%)
  between operations  15.5 us (2%)
    reduce_scatter x1, waiting for transfers between devices, body(): lax.psum_scatter(down_grad.astype(jnp.bfloat16), 'wa', scatter_dimension=...  88 us
    reduce_scatter x1, waiting for transfers between devices, body(): lax.psum_scatter(up_grad.astype(jnp.bfloat16), 'wa', scatter_dimension=0,...  86.2 us
    all_gather x1, waiting for transfers between devices, body(): lax.all_gather(up_weight, 'wa', axis=0, tiled=True)  85.4 us
    all_gather x1, waiting for transfers between devices, body(): lax.all_gather(down_weight, 'wa', axis=0, tiled=True)  82.7 us
    all_gather x1, waiting for transfers between devices, body(): lax.all_gather(qkv_weight, 'wa', axis=0, tiled=True)  58.5 us
    unnamed x17, waiting for transfers between devices  58.1 us
    psum x1, waiting for transfers between devices, body(): lax.psum(owned[0].astype(jnp.bfloat16), 'ctx').astype(jnp.float32)  54 us
    reduce_scatter x1, waiting for transfers between devices, body(): lax.psum_scatter(key_terms.astype(jnp.bfloat16), 'ctx', scatter_dimension...  49.4 us
  transfers between devices with their start and end apart: 15, of which 13 were waited for; matrix products, arithmetic and copies ran while one was open for 10% of the time, Pallas kernels for 0%

commit v1 on v0

--- a/solution.py
+++ b/solution.py
@@ -141,12 +141,30 @@
     vectors,
     cotangent,
 ):
+
+    def define_slabs(patch):
+        mesh_dim = "wa"
+        n = lax.psum(1, mesh_dim)
+        steps_seen = [(no, (no + 1) % n) for no in range(n)]
+        tray = [(no, (no - 1) % n) for no in range(n)]
+        w1, seen_now = ([patch], [patch])
+        for _ in range(n // 2):
+            w1.append(lax.ppermute(w1[-1], mesh_dim, steps_seen))
+        num = 0
+        while num < (n - 1) // 2:
+            seen_now.append(lax.ppermute(seen_now[-1], mesh_dim, tray))
+            num = num + 1
+        long_array = jnp.concatenate([*w1[::-1], *seen_now[1:]], axis=0)
+        return jnp.roll(
+            long_array, shift=(lax.axis_index(mesh_dim) - n // 2) * patch.shape[0], axis=0
+        )
+
     gathered = (
         lax.all_gather(qkv_weight, "wa", axis=0, tiled=True),
         lax.all_gather(out_weight, "wa", axis=0, tiled=True),
         lax.all_gather(up_weight, "wa", axis=0, tiled=True),
         lax.all_gather(up_bias, "wa", axis=0, tiled=True),
-        lax.all_gather(down_weight, "wa", axis=0, tiled=True),
+        define_slabs(down_weight),
         lax.all_gather(proj_weight, "wa", axis=0, tiled=True),
         lax.all_gather(vectors, "wa", axis=1, tiled=True),
     )

time: 953 us -> 909 us (0.954)
  waiting for transfers between devices: 660 us -> 516 us
  blocking collectives: 78.2 us -> 132 us
  matrix products: 78.4 us -> 95.8 us
  local copies, waits for them, and re-layouts: 86.5 us -> 103 us
    all_gather x1, waiting for transfers between devices: 85.4 us -> 0.02 us  [body(): lax.all_gather(up_weight, 'wa', axis=0, tiled=True)]
    all_gather x1 -> x0, waiting for transfers between devices: 82.7 us -> none  [body(): lax.all_gather(down_weight, 'wa', axis=0, tiled=True)]
    all_gather x1, blocking collectives: 13.1 us -> 64.3 us  [body(): lax.all_gather(up_bias, 'wa', axis=0, tiled=True)]
    ppermute x0 -> x3, waiting for transfers between devices: none -> 26.7 us  [the longest x2 26.7 us: define_slabs(): w1.append(lax.ppermute(w1[-1], mesh_dim, steps_seen))]
    all_gather x1, waiting for transfers between devices: 19.9 us -> 0.02 us  [body(): lax.all_gather(key_rows, 'ctx', axis=1, tiled=True)]
    all_gather x1, waiting for transfers between devices: 58.5 us -> 74.3 us  [body(): lax.all_gather(qkv_weight, 'wa', axis=0, tiled=True)]
    unnamed x126 -> x141, local copies, waits for them, and re-layouts: 27.6 us -> 37.2 us
    unnamed x17 -> x16, waiting for transfers between devices: 58.1 us -> 56.7 us
  transfers between devices with their start and end apart: 15 -> 17, of which waited for: 13 -> 11; matrix products, arithmetic and copies ran while one was open for 10% -> 13% of each run, Pallas kernels for 0% -> 0%
where the time goes in v1:
time: 909 us; the launch traced here: 900 us
  waiting for transfers between devices  516 us (57%)
  blocking collectives  132 us (15%)
  local copies, waits for them, and re-layouts  103 us (11%)
  matrix products  95.8 us (11%)
  other arithmetic  32.5 us (4%)
  between operations  15.7 us (2%)
    reduce_scatter x1, waiting for transfers between devices, body(): lax.psum_scatter(down_grad.astype(jnp.bfloat16), 'wa', scatter_dimension=...  88.2 us
    reduce_scatter x1, waiting for transfers between devices, body(): lax.psum_scatter(up_grad.astype(jnp.bfloat16), 'wa', scatter_dimension=0,...  86.1 us
    all_gather x1, waiting for transfers between devices, body(): lax.all_gather(qkv_weight, 'wa', axis=0, tiled=True)  74.3 us
    all_gather x1, blocking collectives, body(): lax.all_gather(up_bias, 'wa', axis=0, tiled=True)  64.3 us
    unnamed x16, waiting for transfers between devices  56.7 us
    psum x1, waiting for transfers between devices, body(): lax.psum(owned[0].astype(jnp.bfloat16), 'ctx').astype(jnp.float32)  54.1 us
    reduce_scatter x1, waiting for transfers between devices, body(): lax.psum_scatter(key_terms.astype(jnp.bfloat16), 'ctx', scatter_dimension...  49.5 us
    unnamed x141, local copies, waits for them, and re-layouts  37.2 us
  transfers between devices with their start and end apart: 17, of which 11 were waited for; matrix products, arithmetic and copies ran while one was open for 13% of the time, Pallas kernels for 0%

profile of v1, /device:TPU:0, one launch (start us, length us, event | category | flops | bytes accessed | tf_op | source)
XLA Modules:
  0.0 899.7 jit_solution(9968083897276049326)
XLA Ops:
  8.0 74.3 %all-gather.8.cloned.1.call-done = bf16[768,2304]{1,0:T(8,128)(2,1)} async-done(((bf16[192,2304]{1,0:T(8,128)(2,1)}), bf16[768,2304]{1,0:T(8,128)(2,1)}) %all-gather.8.cloned.1.call-update) | async-done | bytes 3538960 | tf_op jit(solution)/shard_map/all_gather | solution.py:163
  82.2 3.2 fusion.83
  86.3 13.2 %all-gather = bf16[4,192,8]{1,2,0:T(8,128)(2,1)S(1)} all-gather(bf16[1,192,8]{1,2,0:T(8,128)(2,1)S(1)} %bitcast.248), channel_id=1, replica_groups=mesh['ctx'=8,'wa'=4] {'wa'}, dimensions={0}, use_global_device_ids=true | all-gather | bytes 15360 | tf_op jit(solution)/shard_map/all_gather | solution.py:169
  103.4 26.6 %collective-permute-done = bf16[768,768]{1,0:T(8,128)(2,1)S(1)} collective-permute-done((bf16[768,768]{1,0:T(8,128)(2,1)S(1)}, bf16[768,768]{1,0:T(8,128)(2,1)S(1)}, u32[]{:S(2)}, u32[]{:S(2)}) %collective-permute-start) | collective-permute-done | bytes 1179680 | tf_op jit(solution)/shard_map/ppermute | solution.py:152
  130.0 3.8 collective-permute-start.2
  142.5 64.3 %all-gather.1 = bf16[4,1,768]{2,1,0:T(2,128)(2,1)S(1)} all-gather(bf16[1,1,768]{2,1,0:T(2,128)(2,1)S(1)} %reshape.193), channel_id=1, replica_groups=mesh['ctx'=8,'wa'=4] {'wa'}, dimensions={0}, use_global_device_ids=true | all-gather | bytes 7680 | tf_op jit(solution)/shard_map/all_gather | solution.py:166
  210.5 18.2 %all_gather.31 = bf16[768,128]{1,0:T(8,128)(2,1)} all-gather(bf16[192,128]{1,0:T(8,128)(2,1)} %param.25), channel_id=1, replica_groups=mesh['ctx'=8,'wa'=4] {'wa'}, dimensions={0}, use_global_device_ids=true | all-gather | bytes 245760 | tf_op jit(solution)/shard_map/all_gather | solution.py:168
  233.3 3.6 copy-done.37
  240.4 4.0 reshape.180
  247.0 4.7 copy.70
  251.7 6.2 reshape.179
  257.9 4.3 copy.75
  262.2 21.5 %while.39 = (s32[]{:T(128)}, f32[2,12,128]{2,1,0:T(8,128)S(1)}, f32[2,12,128]{2,1,0:T(8,128)}, pred[2,2,512]{2,1,0:T(4,128)(4,1)}, bf16[2,2,512,12,64]{2,4,3,1,0...) while((s32[]{:T(128)}, f32[2,12,128]{2,1,0:T(8,128)S(1)}, ...), condition=%wide.region_3.4_spmd.clone, body=%wide.region_0.3_spmd.clone.sunk | while | flops 210779136 | bytes 14816444 | solution.py:71
  262.8 4.7 bitcast_reduce_fusion.2
  268.2 4.0 fusion.199
  273.6 4.7 bitcast_reduce_fusion.2
  279.0 4.0 fusion.199
  285.0 11.2 %while.40 = (s32[]{:T(128)}, f32[2,128,12,64]{1,3,2,0:T(8,128)}, bf16[2,2,512,12,64]{2,4,3,1,0:T(8,128)(2,1)}, pred[2,2,512]{2,1,0:T(4,128)(4,1)}, bf16[2,2,512,...) while((s32[]{:T(128)}, f32[2,128,12,64]{1,3,2,0:T(8,128)}, ...), condition=%wide.region_5.6_spmd.clone, body=%wide.region_4.5_spmd.clone.sunk | while | flops 409337856 | bytes 5133419 | solution.py:86
  285.6 4.6 fusion.204
  290.9 4.8 fusion.204
  301.5 6.1 multiply_convert_fusion.1
  307.6 4.7 fusion.159
  321.2 8.2 fusion.162
  338.7 33.7 %while.41 = (s32[]{:T(128)}, f32[2,128,12,64]{1,3,2,0:T(8,128)}, bf16[2,2,512,12,64]{2,4,3,1,0:T(8,128)(2,1)}, bf16[2,2,512,12,64]{2,4,3,1,0:T(8,128)(2,1)}, bf1...) while((s32[]{:T(128)}, f32[2,128,12,64]{1,3,2,0:T(8,128)}, ...), condition=%wide.region_18.19_spmd.clone, body=%wide.region_17.18_spmd.clone.sunk | while | flops 1022754816 | bytes 132275064 | solution.py:122
  351.5 3.9 bitcast_dynamic-update-slice_fusion.5
  364.9 3.4 fusion.216
  368.4 4.0 bitcast_dynamic-update-slice_fusion.5
  372.4 5.1 copy.87
  377.5 3.9 convert_element_type.275
  381.4 4.6 copy.88
  386.1 5.1 copy.85
  391.3 4.1 convert_element_type.272
  395.4 4.8 copy.86
  402.4 30.1 %reduce-scatter.15.cloned.1.call-done = bf16[2,128,768]{2,1,0:T(8,128)(2,1)} async-done(((bf16[2,1024,768]{2,1,0:T(8,128)(2,1)}), bf16[2,128,768]{2,1,0:T(8,128)(2,1)}) %reduce-scatter.15.cloned.1.call-update) | async-done | bytes 393232 | tf_op jit(solution)/shard_map/reduce_scatter | solution.py:259
  432.5 49.5 %reduce-scatter.13.cloned.1.call-done = bf16[2,128,768]{2,1,0:T(8,128)(2,1)} async-done(((bf16[2,1024,768]{2,1,0:T(8,128)(2,1)}), bf16[2,128,768]{2,1,0:T(8,128)(2,1)}) %reduce-scatter.13.cloned.1.call-update) | async-done | bytes 393232 | tf_op jit(solution)/shard_map/reduce_scatter | solution.py:256
  484.5 4.0 copy.104
  491.3 4.5 bitcast_convert_fusion.1
  497.4 3.6 bitcast_convert_fusion
  505.4 49.8 %reduce-scatter.25.cloned.1.call-done = bf16[192,2304]{1,0:T(8,128)(2,1)} async-done(((bf16[768,2304]{1,0:T(8,128)(2,1)}), bf16[192,2304]{1,0:T(8,128)(2,1)}) %reduce-scatter.25.cloned.1.call-update) | async-done | bytes 884752
  557.5 30.1 %reduce-scatter.17.cloned.1.call-done = bf16[192,768]{1,0:T(8,128)(2,1)} async-done(((bf16[768,768]{1,0:T(8,128)(2,1)}), bf16[192,768]{1,0:T(8,128)(2,1)}) %reduce-scatter.17.cloned.1.call-update) | async-done | bytes 294928 | tf_op jit(solution)/shard_map/reduce_scatter | solution.py:289
  587.6 86.1 %reduce-scatter.19.cloned.1.call-done = bf16[192,3072]{1,0:T(8,128)(2,1)} async-done(((bf16[768,3072]{1,0:T(8,128)(2,1)}), bf16[192,3072]{1,0:T(8,128)(2,1)}) %reduce-scatter.19.cloned.1.call-update) | async-done | bytes 1179664 | tf_op jit(solution)/shard_map/reduce_scatter | solution.py:292
  673.7 88.2 %reduce-scatter.21.cloned.1.call-done = bf16[768,768]{1,0:T(8,128)(2,1)} async-done(((bf16[3072,768]{1,0:T(8,128)(2,1)}), bf16[768,768]{1,0:T(8,128)(2,1)}) %reduce-scatter.21.cloned.1.call-update) | async-done | bytes 1179664 | tf_op jit(solution)/shard_map/reduce_scatter | solution.py:298
  763.9 11.2 %all-reduce = bf16[3072]{0:T(1024)(128)(2,1)S(1)} all-reduce(bf16[3072]{0:T(1024)(128)(2,1)S(1)} %copy-done.57), channel_id=7, replica_groups=mesh['ctx'=8,'wa'=4] {'wa'}, use_global_device_ids=true, to_apply=%region_28.29.clone | all-reduce | flops 3072 | bytes 12288
  775.2 4.0 fusion.96
  779.2 5.5 reduce-scatter.27.cloned.1.call-done
  785.5 19.8 %reduce-scatter.23.cloned.1.call-done = bf16[192,128]{1,0:T(8,128)(2,1)} async-done(((bf16[768,128]{1,0:T(8,128)(2,1)}), bf16[192,128]{1,0:T(8,128)(2,1)}) %reduce-scatter.23.cloned.1.call-update) | async-done | bytes 49168 | tf_op jit(solution)/shard_map/reduce_scatter | solution.py:301
  805.4 24.6 %all-reduce.1 = (bf16[768]{0:T(1024)(128)(2,1)S(1)}, bf16[192,128]{1,0:T(8,128)(2,1)S(1)}, bf16[8,192]{1,0:T(8,128)(2,1)S(1)}) all-reduce(bf16[768]{0:T(1024)(128)(2,1)S(1)} %dynamic-slice.1, bf16[192,128]{1,0:T(8,128)(2,1)} %reduce-scatter.23.cloned.1.call-done, bf16[8,192]{1,0:T(8,128)(2,1)S(1)} %copy.107), channel_id=1, replica_groups=mesh['ctx'=8,'wa'=4] {'ctx'}, use_global_device_ids=true, to_apply=%region_29.30 | all-reduce | flops 26880 | bytes 107520 | tf_op jit(solution)/shard_map/psum | solution.py:312
  831.8 54.1 %all-reduce.5.cloned.1.call-done = (bf16[192,2304]{0,1:T(8,128)(2,1)}, bf16[192,768]{1,0:T(8,128)(2,1)}, bf16[192,3072]{1,0:T(8,128)(2,1)}, bf16[768,768]{1,0:T(8,128)(2,1)}) async-done(((bf16[192,2304]{0,1:T(8,128)(2,1)}, bf16[192,768]{1,0:T(8,128)(2,1)}, bf16[192,3072]{1,0:T(8,128)(2,1)}, bf16[768,768]{1,0:T(8,128)(2,1)}), (bf16[192,2304]{0,1:T(8,128)(2,1)}, bf16[192,768]{1,0:T(8,128)(2,1)}, ...) | async-done | bytes 3538960 | tf_op jit(solution)/shard_map/psum | solution.py:309
  (305 shorter events, 107.0 us)
Async XLA Ops:
  7.2 75.1 %all-gather.8.cloned.1.call-start = ((), (), s32[]{:S(2)}) async-start(), calls=%async_computation.8 | async-start | bytes 4423680 | tf_op jit(solution)/shard_map/all_gather | solution.py:163
  7.9 78.4 %copy-start.61 = (bf16[8,192]{1,0:T(8,128)(2,1)S(1)}, bf16[8,192]{1,0:T(8,128)(2,1)}, u32[]{:S(2)}) copy-start(bf16[8,192]{1,0:T(8,128)(2,1)} %param.26) | copy-start | bytes 9220
  7.9 229.3 %all-gather.12.cloned.1.call-start = ((), (), s32[]{:S(2)}) async-start(), calls=%async_computation.10 | async-start | bytes 3538944 | tf_op jit(solution)/shard_map/all_gather | solution.py:190
  85.5 17.8 %copy-start.13 = (bf16[768,768]{1,0:T(8,128)(2,1)S(1)}, bf16[768,768]{1,0:T(8,128)(2,1)}, u32[]{:S(2)}) copy-start(bf16[768,768]{1,0:T(8,128)(2,1)} %param.24) | copy-start | bytes 3538948
  86.3 160.7 %all-gather.10.cloned.1.call-start = ((), (), s32[]{:S(2)}) async-start(), calls=%async_computation.9 | async-start | bytes 3538944 | tf_op jit(solution)/shard_map/all_gather | solution.py:191
  102.6 195.5 %all-gather.14.cloned.1.call-start = ((), (), s32[]{:S(2)}) async-start(), calls=%async_computation.11 | async-start | bytes 1474560 | tf_op jit(solution)/shard_map/all_gather | solution.py:164
  103.2 198.2 %all-gather.16.cloned.1.call-start = ((), (), s32[]{:S(2)}) async-start(), calls=%async_computation.12 | async-start | bytes 5898240 | tf_op jit(solution)/shard_map/all_gather | solution.py:165
  103.3 26.7 %collective-permute-start = (bf16[768,768]{1,0:T(8,128)(2,1)S(1)}, bf16[768,768]{1,0:T(8,128)(2,1)S(1)}, u32[]{:S(2)}, u32[]{:S(2)}) collective-permute-start(bf16[768,768]{1,0:T(8,128)(2,1)S(1)} %copy-done.13), channel_id=1, source_target_pairs={{0,1},{1,2},{2,3},{3,0},{4,5},{5,6},{6,7},{7,4},{8,9},{9,10},{10,1... | collective-permute-start | bytes 3538952 | tf_op jit(solution)/shard_map/ppermute | solution.py:152
  130.0 100.1 %collective-permute-start.1 = (bf16[768,768]{1,0:T(8,128)(2,1)S(1)}, bf16[768,768]{1,0:T(8,128)(2,1)}, u32[]{:S(2)}, u32[]{:S(2)}) collective-permute-start(bf16[768,768]{1,0:T(8,128)(2,1)S(1)} %collective-permute-done), channel_id=1, source_target_pairs={{0,1},{1,2},{2,3},{3,0},{4,5},{5,6},{6,7},{7,4},{8,9},{9,10},{10,1... | collective-permute-start | bytes 3538952 | tf_op jit(solution)/shard_map/ppermute | solution.py:152
  130.0 101.6 %collective-permute-start.2 = (bf16[768,768]{1,0:T(8,128)(2,1)S(1)}, bf16[768,768]{1,0:T(8,128)(2,1)S(1)}, u32[]{:S(2)}, u32[]{:S(2)}) collective-permute-start(bf16[768,768]{1,0:T(8,128)(2,1)S(1)} %copy-done.13), channel_id=1, source_target_pairs={{0,3},{1,0},{2,1},{3,2},{4,7},{5,4},{6,5},{7,6},{8,11},{9,8},{10,9... | collective-permute-start | bytes 3538952 | tf_op jit(solution)/shard_map/ppermute | solution.py:155
  133.8 298.7 %reduce-scatter.15.cloned.1.call-start = ((), (), s32[]{:S(2)}) async-start(), calls=%async_computation.14 | async-start | bytes 3538944 | tf_op jit(solution)/shard_map/reduce_scatter | solution.py:259
  262.8 4.7 copy-start.25
  273.6 4.7 copy-start.25
  285.0 13.2 %copy-start.48 = (f32[768]{0:T(1024)S(1)}, f32[768]{0:T(1024)}, u32[]{:S(2)}) copy-start(f32[768]{0:T(1024)} %get-tuple-element.337) | copy-start | bytes 9220
  296.2 5.2 copy-start.36
  296.2 5.2 copy-start.38
  300.3 31.5 %copy-start.41 = (f32[2,128]{1,0:T(2,128)}, f32[2,128]{1,0:T(2,128)S(1)}, u32[]{:S(2)}) copy-start(f32[2,128]{1,0:T(2,128)S(1)} %broadcast_multiply_fusion.5) | copy-start | bytes 3076
  301.4 6.2 copy-start.50
  301.4 6.1 copy-start.6
  301.5 6.1 copy-start.60
  307.5 4.7 copy-start.15
  307.6 5.6 copy-start.28
  307.6 5.6 copy-start.39
  307.6 5.6 copy-start.46
  318.8 10.6 %slice-start = ((s8[4718592]{0:T(1024)(128)(4,1)}), s8[4194304]{0:T(1024)(128)(4,1)S(1)}, s32[]{:S(2)}) async-start(s8[4718592]{0:T(1024)(128)(4,1)} %bitcast.249), calls=%async_computation.22 | async-start | bytes 8388608
  321.2 8.2 copy-start.19
  321.2 8.2 copy-start.7
  321.2 8.2 copy-start.51
  321.2 8.2 slice-start.1
  331.8 6.9 copy-start.34
  338.9 4.3 copy-start.22
  338.9 4.3 copy-start.43
  338.9 4.3 copy-start.49
  340.5 5.3 copy-start.2
  357.1 5.3 copy-start.2
  386.1 95.9 %reduce-scatter.13.cloned.1.call-start = ((), (), s32[]{:S(2)}) async-start(), calls=%async_computation.13 | async-start | bytes 3538944 | tf_op jit(solution)/shard_map/reduce_scatter | solution.py:256
  400.2 155.0 %reduce-scatter.25.cloned.1.call-start = ((), (), s32[]{:S(2)}) async-start(), calls=%async_computation.19 | async-start | bytes 4423680
  488.6 99.1 %reduce-scatter.17.cloned.1.call-start = ((), (), s32[]{:S(2)}) async-start(), calls=%async_computation.15 | async-start | bytes 1474560 | tf_op jit(solution)/shard_map/reduce_scatter | solution.py:289
  491.3 182.4 %reduce-scatter.19.cloned.1.call-start = ((), (), s32[]{:S(2)}) async-start(), calls=%async_computation.16 | async-start | bytes 5898240 | tf_op jit(solution)/shard_map/reduce_scatter | solution.py:292
  495.8 266.0 %reduce-scatter.21.cloned.1.call-start = ((), (), s32[]{:S(2)}) async-start(), calls=%async_computation.17 | async-start | bytes 5898240 | tf_op jit(solution)/shard_map/reduce_scatter | solution.py:298
  501.2 283.5 %reduce-scatter.27.cloned.1.call-start = ((), (), s32[]{:S(2)}) async-start(), calls=%async_computation.20 | async-start | bytes 245760
  503.1 302.3 %reduce-scatter.23.cloned.1.call-start = ((), (), s32[]{:S(2)}) async-start(), calls=%async_computation.18 | async-start | bytes 245760 | tf_op jit(solution)/shard_map/reduce_scatter | solution.py:301
  505.3 256.6 %copy-start.67 = (u32[32]{0:T(128)S(1)}, u32[32]{0:T(128)}, u32[]{:S(2)}) copy-start(u32[32]{0:T(128)} %constant.123) | copy-start | bytes 388
  505.3 258.6 %copy-start.57 = (bf16[3072]{0:T(1024)(128)(2,1)S(1)}, bf16[3072]{0:T(1024)(128)(2,1)}, u32[]{:S(2)}) copy-start(bf16[3072]{0:T(1024)(128)(2,1)} %get-tuple-element.415) | copy-start | bytes 18436
  505.3 269.9 %copy-start.33 = (bf16[2,128,768]{2,1,0:T(8,128)(2,1)S(1)}, bf16[2,128,768]{2,1,0:T(8,128)(2,1)}, u32[]{:S(2)}) copy-start(bf16[2,128,768]{2,1,0:T(8,128)(2,1)} %copy.89) | copy-start | bytes 1179652
  505.3 269.9 %copy-start.66 = (bf16[2,128,768]{2,1,0:T(8,128)(2,1)S(1)}, bf16[2,128,768]{2,1,0:T(8,128)(2,1)}, u32[]{:S(2)}) copy-start(bf16[2,128,768]{2,1,0:T(8,128)(2,1)} %reduce-scatter.13.cloned.1.call-done) | copy-start | bytes 1179652
  505.3 380.5 %all-reduce.5.cloned.1.call-start = ((), (), s32[]{:S(2)}) async-start(), calls=%async_computation.21 | async-start | bytes 7667712 | tf_op jit(solution)/shard_map/psum | solution.py:309
  885.9 4.7 copy-start.27
  (50 other events, 111.5 us)
Sparse Core Ops, SparseCore 0:
  9.6 72.6 all-gather.7
  86.4 30.7 all-gather.11
  119.7 32.2 all-gather.9
  153.4 41.7 all-gather.13
  196.6 95.0 all-gather.15
  386.2 46.2 reduce-scatter.14
  435.9 46.0 reduce-scatter.12
  488.7 66.4 reduce-scatter.24
  558.1 29.4 reduce-scatter.16
  589.8 83.8 reduce-scatter.18
  676.0 85.7 reduce-scatter.20
  764.5 20.1 reduce-scatter.26
  787.5 17.7 reduce-scatter.22
  809.5 76.2 all-reduce.4
